TPU v7x, 32 devices: a whole 2x2x4 slice. The times are simulated.
32 devices in a mesh: elec: 4 (over y, core), pix: 8 (over z, x).
Axes of the slice: x: 2, y: 2, z: 4, core: 2. Of those that a mesh axis runs over, the one named last changes fastest.
Arguments:
- wavefronts: bfloat16 [1536, 2, 320, 256], P('elec', None, 'pix'), may hold values from -40 to 40, as said below
- trial_modes: float32 [2, 32, 320, 256], P(None, None, 'pix'), may hold values from -6 to 6
Outputs:
- sample_modes: float32 [2, 32, 320, 256], P(None, 'elec', None, 'pix')
Inputs may be any that keep to these rules, and one draw needn't show every extreme that they name: `wavefronts`: field samples of each electron's wavefront.
All inputs are finite; a program needn't handle non-finite values.
Results may differ from a plain program's by a relative error of at most 0.0075.
Values may be sent and summed in bfloat16 or wider, within the bound.
A program may use at most 128 MiB of HBM per device.

v0:
```python
import math
import jax
import jax.numpy as jnp
from jax import lax
from jax.sharding import PartitionSpec as P

ITERS = 2
NS_STEPS = 8
HIGH = lax.Precision.HIGHEST


def project(wave_re, wave_im, modes_low):
    stacked = modes_low.reshape(-1, modes_low.shape[2])
    swapped = jnp.concatenate([-modes_low[1], modes_low[0]], axis=0)
    contract = (((1,), (1,)), ((), ()))
    real_side = lax.dot_general(wave_re, stacked, contract, preferred_element_type=jnp.float32)
    imag_side = lax.dot_general(wave_im, swapped, contract, preferred_element_type=jnp.float32)
    return real_side + imag_side


def covariance(waves, projected, mode_count):
    pixels = waves.shape[1] // 2
    width = projected.shape[1]
    upper = projected.astype(jnp.bfloat16)
    lower = (projected - upper.astype(jnp.float32)).astype(jnp.bfloat16)
    both = jnp.concatenate([upper, lower], axis=1)
    stacked = lax.dot_general(
        both, waves, (((0,), (0,)), ((), ())), preferred_element_type=jnp.float32
    )
    blocks = stacked[:width] + stacked[width:]
    real_part = blocks[:mode_count, :pixels] + blocks[mode_count:, pixels:]
    imag_part = blocks[mode_count:, :pixels] - blocks[:mode_count, pixels:]
    return jnp.stack([real_part, imag_part])


def gram_matrix(fields):
    flat = fields.reshape(-1, fields.shape[2])
    return jnp.dot(flat, flat.T, precision=HIGH)


def lowdin(gram_raw, mode_count):
    gram_re = gram_raw[:mode_count, :mode_count] + gram_raw[mode_count:, mode_count:]
    gram_im = gram_raw[:mode_count, mode_count:] - gram_raw[mode_count:, :mode_count]
    embedded = jnp.concatenate(
        [jnp.concatenate([gram_re, -gram_im], 1), jnp.concatenate([gram_im, gram_re], 1)], 0
    )
    trace_value = jnp.trace(embedded)
    scaled = embedded / trace_value
    identity = jnp.eye(2 * mode_count, dtype=embedded.dtype)
    inverse_root = identity
    for iteration in range(NS_STEPS):
        correction = 1.5 * identity - 0.5 * jnp.dot(inverse_root, scaled, precision=HIGH)
        scaled = jnp.dot(scaled, correction, precision=HIGH)
        inverse_root = jnp.dot(correction, inverse_root, precision=HIGH)
    return (inverse_root / jnp.sqrt(trace_value)).T


def rotate(rotation, fields):
    flat = fields.reshape(-1, fields.shape[2])
    return jnp.dot(rotation, flat, precision=HIGH).reshape(fields.shape)


def dft_table(length):
    index = jnp.arange(length, dtype=jnp.int32)
    product = index[:, None] * index[None, :] % length
    angle = 2.0 * math.pi / length * product.astype(jnp.float32)
    return (jnp.cos(angle), -jnp.sin(angle))


def chirp_phase(row_pos, col_pos, row_total, col_total, factor):
    row_term = (row_pos - row_total / 2.0) ** 2 / row_total
    col_term = (col_pos - col_total / 2.0) ** 2 / col_total
    angle = math.pi * factor * (row_term[:, None] + col_term[None, :])
    return (jnp.cos(angle), jnp.sin(angle))


def column_section(field, row_pos, row_total, col_total):
    col_pos = jnp.arange(col_total, dtype=jnp.float32)
    chirp_re, chirp_im = chirp_phase(row_pos, col_pos, row_total, col_total, 0.5)
    launch_re = chirp_re * field[0] - chirp_im * field[1]
    launch_im = chirp_re * field[1] + chirp_im * field[0]
    table_re, table_im = dft_table(col_total)
    spec_re = jnp.einsum("mry,yv->mrv", launch_re, table_re, precision=HIGH) - jnp.einsum(
        "mry,yv->mrv", launch_im, table_im, precision=HIGH
    )
    spec_im = jnp.einsum("mry,yv->mrv", launch_re, table_im, precision=HIGH) + jnp.einsum(
        "mry,yv->mrv", launch_im, table_re, precision=HIGH
    )
    return jnp.stack([spec_re, spec_im])


def row_section(spectrum, col_pos, row_total, col_total):
    table_re, table_im = dft_table(row_total)
    out_re = jnp.einsum("ux,mxv->muv", table_re, spectrum[0], precision=HIGH) - jnp.einsum(
        "ux,mxv->muv", table_im, spectrum[1], precision=HIGH
    )
    out_im = jnp.einsum("ux,mxv->muv", table_re, spectrum[1], precision=HIGH) + jnp.einsum(
        "ux,mxv->muv", table_im, spectrum[0], precision=HIGH
    )
    row_pos = jnp.arange(row_total, dtype=jnp.float32)
    chirp_re, chirp_im = chirp_phase(row_pos, col_pos, row_total, col_total, 0.25)
    return jnp.stack([chirp_re * out_re - chirp_im * out_im, chirp_re * out_im + chirp_im * out_re])


def pixel_sum(partial_value):
    return lax.psum(partial_value, "pix")


def shards(wavefronts, trial_modes):
    electrons_dev, _, rows_dev, cols = wavefronts.shape
    mode_count = trial_modes.shape[1]
    pixels = rows_dev * cols
    groups = lax.axis_size("elec")
    mode_share = mode_count // groups
    waves = wavefronts.reshape(electrons_dev, 2 * pixels)
    wave_re = waves[:, :pixels]
    wave_im = waves[:, pixels:]
    modes = trial_modes.reshape(2, mode_count, pixels)
    projected_part = project(wave_re, wave_im, modes.astype(jnp.bfloat16))
    share_low = None
    share_modes = None
    for iteration in range(ITERS):
        if iteration > 0:
            projected_part = project(
                wave_re, wave_im, lax.all_gather(share_low, "elec", axis=2, tiled=True)
            )
        projected = pixel_sum(projected_part)
        applied_share = lax.psum_scatter(
            covariance(waves, projected, mode_count), "elec", scatter_dimension=2, tiled=True
        )
        gram_total = lax.psum(gram_matrix(applied_share), ("elec", "pix"))
        share_modes = rotate(lowdin(gram_total, mode_count), applied_share)
        share_low = share_modes.astype(jnp.bfloat16)
    local_modes = lax.all_to_all(share_modes, "elec", split_axis=1, concat_axis=2, tiled=True)
    field = local_modes.reshape(2, mode_share, rows_dev, cols)
    pix_count = lax.axis_size("pix")
    row_total = rows_dev * pix_count
    row_pos = (lax.axis_index("pix") * rows_dev + jnp.arange(rows_dev, dtype=jnp.int32)).astype(
        jnp.float32
    )
    spectrum = column_section(field, row_pos, row_total, cols)
    column_block = lax.all_to_all(spectrum, "pix", split_axis=3, concat_axis=2, tiled=True)
    col_width = column_block.shape[3]
    col_pos = (lax.axis_index("pix") * col_width + jnp.arange(col_width, dtype=jnp.int32)).astype(
        jnp.float32
    )
    return row_section(column_block, col_pos, row_total, cols)


def solution(mesh):
    in_specs = (P("elec", None, "pix", None), P(None, None, "pix", None))
    out_specs = P(None, "elec", None, "pix")
    return jax.shard_map(shards, mesh=mesh, in_specs=in_specs, out_specs=out_specs, check_vma=False)
```

profile of v0, /device:TPU:0, one launch (start us, length us, event | category | flops | bytes accessed | tf_op | source)
XLA Modules:
  0.0 470.5 jit_solution(15132005642279305516)
XLA Ops:
  6.5 11.1 %copy.19 = bf16[48,8,80,256]{3,1,2,0:T(8,128)(2,1)S(1)} copy(bf16[48,8,80,256]{3,2,1,0:T(8,128)(2,1)} %bitcast.196) | data formatting | bytes 31457280
  18.4 2.5 fusion.6
  21.0 2.2 copy-done
  23.2 3.2 fusion.27
  26.4 73.0 %all-reduce.3.cloned.1.call-done = f32[384,64]{0,1:T(8,128)} async-done(((f32[384,64]{0,1:T(8,128)}), f32[384,64]{0,1:T(8,128)}) %all-reduce.3.cloned.1.call-update) | async-done | bytes 98320 | tf_op jit(solution)/shard_map/psum | solution.py:106
  99.5 1.0 subtract_convert_fusion.1
  100.4 7.0 %fusion.98 = f32[128,20480]{1,0:T(8,128)S(1)} fusion(bf16[384,20480]{1,0:T(8,128)(2,1)} %bitcast.192, bf16[384,64]{0,1:T(8,128)(2,1)S(1)} %get-tuple-element.11, bf16[384,64]{0,1:T(8,128)(2,1)S(1)} %get-tuple-element.12), kind=kOutput, calls=%fused_computation.123 | convolution fusion | flops 2013462528 | bytes 26312704 | tf_op jit(solution)/shard_map/dot_general | solution.py:27
  108.3 1.7 pad_maximum_fusion
  110.0 33.6 %reduce-scatter.3.cloned.1.call-done = f32[2,32,2560]{2,1,0:T(8,128)} async-done(((f32[2,32,10240]{2,1,0:T(8,128)}), f32[2,32,2560]{2,1,0:T(8,128)}) %reduce-scatter.3.cloned.1.call-update) | async-done | bytes 655376 | tf_op jit(solution)/shard_map/reduce_scatter | solution.py:128
  143.7 2.0 fusion.152
  145.7 39.4 %psum.29 = f32[64,64]{1,0:T(8,128)S(1)} all-reduce(f32[64,64]{1,0:T(8,128)S(1)} %fusion.152), channel_id=1, replica_groups=mesh['elec'=4,'pix'=8] {'elec','pix'}, use_global_device_ids=true, to_apply=%region_2.0 | all-reduce | flops 4096 | bytes 32768 | tf_op jit(solution)/shard_map/psum | solution.py:131
  185.9 0.9 fusion.53
  186.8 0.9 fusion.112
  192.0 1.4 convolution_convert_fusion
  193.9 18.5 %all-gather.2.cloned.1.call-done = bf16[2,32,10240]{2,1,0:T(8,128)(2,1)} async-done(((bf16[2,32,2560]{2,1,0:T(8,128)(2,1)}), bf16[2,32,10240]{2,1,0:T(8,128)(2,1)}) %all-gather.2.cloned.1.call-update) | async-done | bytes 1310736 | tf_op jit(solution)/shard_map/all_gather | solution.py:125
  212.4 1.4 fusion.54
  213.8 5.9 %fusion = f32[64,384]{1,0:T(8,128)S(1)} fusion(bf16[384,20480]{1,0:T(8,128)(2,1)} %bitcast.193, bf16[32,10240]{1,0:T(8,128)(2,1)S(1)} %get-tuple-element.20, bf16[32,10240]{1,0:T(8,128)(2,1)S(1)} %get-tuple-element.19), kind=kOutput, calls=%fused_computation | convolution fusion | flops 505937920 | bytes 9273344 | tf_op jit(solution)/shard_map/dot_general | solution.py:17
  219.7 6.4 %fusion.35 = f32[384,64]{0,1:T(8,128)} fusion(f32[64,384]{1,0:T(8,128)S(1)} %fusion, bf16[64,10240]{1,0:T(8,128)(2,1)S(1)} %bitcast.208, bf16[384,20480]{1,0:T(8,128)(2,1)} %bitcast.194), kind=kOutput, calls=%fused_computation.38 | convolution fusion | flops 503341056 | bytes 9371648 | tf_op jit(solution)/shard_map/dot_general | solution.py:16
  226.2 70.3 %all-reduce.5.cloned.1.call-done = f32[384,64]{0,1:T(8,128)} async-done(((f32[384,64]{0,1:T(8,128)}), f32[384,64]{0,1:T(8,128)}) %all-reduce.5.cloned.1.call-update) | async-done | bytes 98320 | tf_op jit(solution)/shard_map/psum | solution.py:106
  296.5 1.0 subtract_convert_fusion
  297.5 7.0 %fusion.102 = f32[128,20480]{1,0:T(8,128)S(1)} fusion(bf16[384,20480]{1,0:T(8,128)(2,1)} %bitcast.195, bf16[384,64]{0,1:T(8,128)(2,1)S(1)} %get-tuple-element.7, bf16[384,64]{0,1:T(8,128)(2,1)S(1)} %get-tuple-element.8), kind=kOutput, calls=%fused_computation.127 | convolution fusion | flops 2013462528 | bytes 26312704 | tf_op jit(solution)/shard_map/dot_general | solution.py:27
  305.3 1.7 pad_maximum_fusion.1
  307.0 33.7 %reduce-scatter.5.cloned.1.call-done = f32[2,32,2560]{2,1,0:T(8,128)} async-done(((f32[2,32,10240]{2,1,0:T(8,128)}), f32[2,32,2560]{2,1,0:T(8,128)}) %reduce-scatter.5.cloned.1.call-update) | async-done | bytes 655376 | tf_op jit(solution)/shard_map/reduce_scatter | solution.py:128
  340.7 2.0 fusion.165
  342.8 39.4 %psum.31 = f32[64,64]{1,0:T(8,128)S(1)} all-reduce(f32[64,64]{1,0:T(8,128)S(1)} %fusion.165), channel_id=1, replica_groups=mesh['elec'=4,'pix'=8] {'elec','pix'}, use_global_device_ids=true, to_apply=%region_6.7 | all-reduce | flops 4096 | bytes 32768 | tf_op jit(solution)/shard_map/psum | solution.py:131
  383.0 0.9 fusion.45
  383.8 0.9 fusion.113
  389.7 1.3 copy.11
  391.1 3.7 all-to-all-start
  395.1 9.9 %all-to-all-done = f32[2,32,2560]{2,0,1:T(2,128)S(1)} async-done(((f32[2,32,2560]{2,0,1:T(2,128)}), f32[2,32,2560]{2,0,1:T(2,128)S(1)}, u32[]{:S(2)}, u32[]{:S(2)}) %all-to-all-start) | async-done | bytes 655392 | tf_op jit(solution)/shard_map/all_to_all | solution.py:134
  406.3 1.4 fusion.76
  407.7 1.4 fusion.72
  409.1 1.4 fusion.21
  410.6 1.4 fusion.20
  412.0 1.3 copy.14
  413.3 2.9 reshape.190
  416.2 5.2 %all-to-all-start.1 = ((f32[8,1,20480]{2,1,0:T(1,128)}), f32[8,1,20480]{2,1,0:T(1,128)S(1)}, u32[]{:S(2)}, u32[]{:S(2)}) async-start(f32[8,1,20480]{2,1,0:T(1,128)} %reshape.190), calls=%async_computation.3 | async-start | bytes 1310720 | tf_op jit(solution)/shard_map/all_to_all | solution.py:142
  421.7 16.7 %all-to-all-done.1 = f32[8,1,20480]{2,1,0:T(1,128)S(1)} async-done(((f32[8,1,20480]{2,1,0:T(1,128)}), f32[8,1,20480]{2,1,0:T(1,128)S(1)}, u32[]{:S(2)}, u32[]{:S(2)}) %all-to-all-start.1) | async-done | bytes 655392 | tf_op jit(solution)/shard_map/all_to_all | solution.py:142
  438.9 2.2 reduce
  441.1 3.0 reshape.191
  444.1 2.4 copy.18
  446.5 1.7 fusion.148
  448.3 1.9 copy.17
  450.5 2.8 fusion.59
  454.1 2.8 fusion.61
  456.9 2.8 fusion.18
  459.7 2.9 subtract_bitcast_fusion
  462.6 0.9 pad_maximum_fusion.2
  (93 shorter events, 15.6 us)
Async XLA Ops:
  6.5 92.9 %all-reduce.3.cloned.1.call-start = ((), (), s32[]{:S(2)}) async-start(), calls=%async_computation.4 | async-start | bytes 196608 | tf_op jit(solution)/shard_map/psum | solution.py:106
  6.5 11.1 %copy-start.4 = (f32[2,32,40,256]{3,2,1,0:T(8,128)S(1)}, f32[2,32,40,256]{3,2,1,0:T(8,128)}, u32[]{:S(2)}) copy-start(f32[2,32,40,256]{3,2,1,0:T(8,128)} %param.3) | copy-start | bytes 7864324
  17.7 5.5 %copy-start = (bf16[48,8,80,256]{3,1,2,0:T(8,128)(2,1)}, bf16[48,8,80,256]{3,1,2,0:T(8,128)(2,1)S(1)}, u32[]{:S(2)}) copy-start(bf16[48,8,80,256]{3,1,2,0:T(8,128)(2,1)S(1)} %copy.19) | copy-start | bytes 47185924
  26.4 117.3 %reduce-scatter.3.cloned.1.call-start = ((), (), s32[]{:S(2)}) async-start(), calls=%async_computation.5 | async-start | bytes 3276800 | tf_op jit(solution)/shard_map/reduce_scatter | solution.py:128
  110.0 102.5 %all-gather.2.cloned.1.call-start = ((), (), s32[]{:S(2)}) async-start(), calls=%async_computation.6 | async-start | bytes 1638400 | tf_op jit(solution)/shard_map/all_gather | solution.py:125
  143.7 48.3 %copy-start.2 = (f32[2,32,2560]{2,1,0:T(8,128)S(1)}, f32[2,32,2560]{2,1,0:T(8,128)}, u32[]{:S(2)}) copy-start(f32[2,32,2560]{2,1,0:T(8,128)} %reduce-scatter.3.cloned.1.call-done) | copy-start | bytes 1966084
  193.4 103.1 %all-reduce.5.cloned.1.call-start = ((), (), s32[]{:S(2)}) async-start(), calls=%async_computation.7 | async-start | bytes 196608 | tf_op jit(solution)/shard_map/psum | solution.py:106
  213.8 5.9 %copy-start.5 = (bf16[2,32,10240]{2,1,0:T(8,128)(2,1)S(1)}, bf16[2,32,10240]{2,1,0:T(8,128)(2,1)}, u32[]{:S(2)}) copy-start(bf16[2,32,10240]{2,1,0:T(8,128)(2,1)} %all-gather.2.cloned.1.call-done) | copy-start | bytes 3932164
  226.2 114.6 %reduce-scatter.5.cloned.1.call-start = ((), (), s32[]{:S(2)}) async-start(), calls=%async_computation.8 | async-start | bytes 3276800 | tf_op jit(solution)/shard_map/reduce_scatter | solution.py:128
  340.7 48.3 %copy-start.1 = (f32[2,32,2560]{2,1,0:T(8,128)S(1)}, f32[2,32,2560]{2,1,0:T(8,128)}, u32[]{:S(2)}) copy-start(f32[2,32,2560]{2,1,0:T(8,128)} %reduce-scatter.5.cloned.1.call-done) | copy-start | bytes 1966084
  391.1 13.9 %all-to-all-start = ((f32[2,32,2560]{2,0,1:T(2,128)}), f32[2,32,2560]{2,0,1:T(2,128)S(1)}, u32[]{:S(2)}, u32[]{:S(2)}) async-start(f32[2,32,2560]{2,0,1:T(2,128)} %copy.11), calls=%async_computation.2 | async-start | bytes 1310720 | tf_op jit(solution)/shard_map/all_to_all | solution.py:134
  416.2 22.2 %all-to-all-start.1 = ((f32[8,1,20480]{2,1,0:T(1,128)}), f32[8,1,20480]{2,1,0:T(1,128)S(1)}, u32[]{:S(2)}, u32[]{:S(2)}) async-start(f32[8,1,20480]{2,1,0:T(1,128)} %reshape.190), calls=%async_computation.3 | async-start | bytes 1310720 | tf_op jit(solution)/shard_map/all_to_all | solution.py:142
  448.3 5.0 %copy-start.3 = (f32[1,8,8,40,32]{4,2,3,1,0:T(8,128)S(1)}, f32[1,8,8,40,32]{4,2,3,1,0:T(8,128)}, u32[]{:S(2)}) copy-start(f32[1,8,8,40,32]{4,2,3,1,0:T(8,128)} %get-tuple-element.18) | copy-start | bytes 983044
Sparse Core Ops, SparseCore 0:
  26.5 72.8 all-reduce.2
  110.1 33.5 reduce-scatter.2
  193.5 18.8 all-gather.1
  226.3 70.1 all-reduce.4
  307.2 33.5 reduce-scatter.4
where the time goes:
time: 479 us; the launch traced here: 470 us
  waiting for transfers between devices  256 us (53%)
  blocking collectives  78.9 us (16%)
  matrix products  65.6 us (14%)
  local copies, waits for them, and re-layouts  31.3 us (7%)
  between operations  15.7 us (3%)
  other arithmetic  13.7 us (3%)
  starting transfers between devices  9.51 us (2%)
    psum x2, waiting for transfers between devices, pixel_sum(): return lax.psum(partial_value, 'pix')  143 us
    psum x2, blocking collectives, shards(): gram_total = lax.psum(gram_matrix(applied_share), ('elec', 'pix'))  78.9 us
    reduce_scatter x2, waiting for transfers between devices, shards(): lax.psum_scatter(covariance(waves, projected, mode_count), 'elec', scatte...  67.3 us
    unnamed x18, local copies, waits for them, and re-layouts  19.7 us
    all_gather x1, waiting for transfers between devices, shards(): lax.all_gather(share_low, 'elec', axis=2, tiled=True)  18.5 us
    all_to_all x1, waiting for transfers between devices, shards(): lax.all_to_all(spectrum, 'pix', split_axis=3, concat_axis=2, tiled=True)  16.7 us
    dot_general x2, matrix products, covariance(): lax.dot_general(both, waves, (((0,), (0,)), ((), ())), preferred_element_...  14.1 us
    all_to_all x1, waiting for transfers between devices, shards(): lax.all_to_all(share_modes, 'elec', split_axis=1, concat_axis=2, tiled=True)  9.93 us
  transfers between devices with their start and end apart: 7, of which 7 were waited for; matrix products, arithmetic and copies ran while one was open for 0% of the time, Pallas kernels for 0%

commit v1 on v0

--- a/solution.py
+++ b/solution.py
@@ -7,6 +7,12 @@
 ITERS = 2
 NS_STEPS = 8
 HIGH = lax.Precision.HIGHEST
+
+
+def summed_here(array, axis):
+    shards = lax.all_gather(array, axis, axis=0, tiled=False)
+    total = shards.sum(axis=0)
+    return total
 
 
 def project(wave_re, wave_im, modes_low):
@@ -103,7 +109,7 @@
 
 
 def pixel_sum(partial_value):
-    return lax.psum(partial_value, "pix")
+    return summed_here(partial_value, "pix")
 
 
 def shards(wavefronts, trial_modes):

time: 479 us -> 405 us (0.85)
  waiting for transfers between devices: 256 us -> 116 us
  blocking collectives: 78.9 us -> 145 us
  other arithmetic: 13.7 us -> 20.2 us
    psum x2 -> x0, waiting for transfers between devices: 143 us -> none  [pixel_sum(): return lax.psum(partial_value, 'pix')]
    all_gather x0 -> x2, blocking collectives: none -> 66.1 us  [summed_here(): shards = lax.all_gather(array, axis, axis=0, tiled=False)]
    add x2, other arithmetic: 1.05 us -> 9.16 us  [covariance(): blocks = stacked[:width] + stacked[width:]]
    unnamed x18 -> x26, local copies, waits for them, and re-layouts: 19.7 us -> 17.9 us
  transfers between devices with their start and end apart: 7 -> 5, of which waited for: 7 -> 5; matrix products, arithmetic and copies ran while one was open for 0% -> 0% of each run, Pallas kernels for 0% -> 0%
where the time goes in v1:
time: 405 us; the launch traced here: 398 us
  blocking collectives  145 us (36%)
  waiting for transfers between devices  116 us (29%)
  matrix products  62.7 us (15%)
  local copies, waits for them, and re-layouts  29.2 us (7%)
  other arithmetic  20.2 us (5%)
  between operations  15.5 us (4%)
  starting transfers between devices  9.4 us (2%)
    psum x2, blocking collectives, shards(): gram_total = lax.psum(gram_matrix(applied_share), ('elec', 'pix'))  79.1 us
    reduce_scatter x2, waiting for transfers between devices, shards(): lax.psum_scatter(covariance(waves, projected, mode_count), 'elec', scatte...  70 us
    all_gather x2, blocking collectives, summed_here(): shards = lax.all_gather(array, axis, axis=0, tiled=False)  66.1 us
    all_gather x1, waiting for transfers between devices, shards(): lax.all_gather(share_low, 'elec', axis=2, tiled=True)  19 us
    unnamed x26, local copies, waits for them, and re-layouts  17.9 us
    all_to_all x1, waiting for transfers between devices, shards(): lax.all_to_all(spectrum, 'pix', split_axis=3, concat_axis=2, tiled=True)  16.7 us
    dot_general x2, matrix products, covariance(): lax.dot_general(both, waves, (((0,), (0,)), ((), ())), preferred_element_...  11.1 us
    all_to_all x1, waiting for transfers between devices, shards(): lax.all_to_all(share_modes, 'elec', split_axis=1, concat_axis=2, tiled=True)  9.93 us
  transfers between devices with their start and end apart: 5, of which 5 were waited for; matrix products, arithmetic and copies ran while one was open for 0% of the time, Pallas kernels for 0%

profile of v1, /device:TPU:0, one launch (start us, length us, event | category | flops | bytes accessed | tf_op | source)
XLA Modules:
  0.0 397.8 jit_solution(4791633833057056039)
XLA Ops:
  6.5 11.1 %copy.19 = bf16[48,8,80,256]{3,1,2,0:T(8,128)(2,1)S(1)} copy(bf16[48,8,80,256]{3,2,1,0:T(8,128)(2,1)} %bitcast.208) | data formatting | bytes 31457280
  18.4 2.5 fusion.6
  21.0 2.6 fusion.27
  23.5 33.8 %all-gather = f32[3072,64]{0,1:T(8,128)S(1)} all-gather(f32[384,64]{0,1:T(8,128)S(1)} %fusion.27), channel_id=2, replica_groups=mesh['elec'=4,'pix'=8] {'pix'}, dimensions={0}, use_global_device_ids=true | all-gather | bytes 884736 | tf_op jit(solution)/shard_map/all_gather | solution.py:13
  57.7 5.6 %fusion.98 = f32[128,20480]{1,0:T(8,128)} fusion(bf16[384,20480]{1,0:T(8,128)(2,1)S(1)} %bitcast.202, bf16[384,64]{0,1:T(8,128)(2,1)S(1)} %get-tuple-element.11, bf16[384,64]{0,1:T(8,128)(2,1)S(1)} %get-tuple-element.12), kind=kOutput, calls=%fused_computation.125 | convolution fusion | flops 2013462528 | bytes 26312704 | tf_op jit(solution)/shard_map/dot_general | solution.py:33
  63.3 4.6 %slice_add_fusion.1 = f32[64,20480]{1,0:T(8,128)S(1)} fusion(f32[128,20480]{1,0:T(8,128)} %fusion.98), kind=kLoop, calls=%fused_computation.9 | loop fusion | flops 1310720 | bytes 15728640 | tf_op jit(solution)/shard_map/add | solution.py:36
  68.2 1.7 pad_maximum_fusion
  69.9 35.6 %reduce-scatter.3.cloned.1.call-done = f32[2,32,2560]{2,1,0:T(8,128)} async-done(((f32[2,32,10240]{2,1,0:T(8,128)}), f32[2,32,2560]{2,1,0:T(8,128)}) %reduce-scatter.3.cloned.1.call-update) | async-done | bytes 655376 | tf_op jit(solution)/shard_map/reduce_scatter | solution.py:134
  105.5 2.0 fusion.152
  107.4 39.6 %psum.14 = f32[64,64]{1,0:T(8,128)S(1)} all-reduce(f32[64,64]{1,0:T(8,128)S(1)} %fusion.152), channel_id=1, replica_groups=mesh['elec'=4,'pix'=8] {'elec','pix'}, use_global_device_ids=true, to_apply=%region_2.0 | all-reduce | flops 4096 | bytes 32768 | tf_op jit(solution)/shard_map/psum | solution.py:137
  147.8 0.9 fusion.53
  148.7 0.9 fusion.112
  153.9 2.6 convolution_convert_fusion
  156.6 19.0 %all-gather.4.cloned.1.call-done = bf16[2,32,10240]{2,1,0:T(8,128)(2,1)} async-done(((bf16[2,32,2560]{2,1,0:T(8,128)(2,1)}), bf16[2,32,10240]{2,1,0:T(8,128)(2,1)}) %all-gather.4.cloned.1.call-update) | async-done | bytes 1310736 | tf_op jit(solution)/shard_map/all_gather | solution.py:131
  175.6 1.4 fusion.54
  177.0 5.9 %fusion = f32[64,384]{1,0:T(8,128)S(1)} fusion(bf16[384,20480]{1,0:T(8,128)(2,1)} %bitcast.203, bf16[32,10240]{1,0:T(8,128)(2,1)S(1)} %get-tuple-element.20, bf16[32,10240]{1,0:T(8,128)(2,1)S(1)} %get-tuple-element.19), kind=kOutput, calls=%fused_computation | convolution fusion | flops 505937920 | bytes 9273344 | tf_op jit(solution)/shard_map/dot_general | solution.py:23
  183.0 5.9 %fusion.35 = f32[384,64]{0,1:T(8,128)S(1)} fusion(f32[64,384]{1,0:T(8,128)S(1)} %fusion, bf16[64,10240]{1,0:T(8,128)(2,1)S(1)} %bitcast.222, bf16[384,20480]{1,0:T(8,128)(2,1)} %bitcast.204), kind=kOutput, calls=%fused_computation.38 | convolution fusion | flops 503341056 | bytes 9371648 | tf_op jit(solution)/shard_map/dot_general | solution.py:22
  188.9 32.3 %all-gather.1 = f32[3072,64]{0,1:T(8,128)S(1)} all-gather(f32[384,64]{0,1:T(8,128)S(1)} %fusion.35), channel_id=3, replica_groups=mesh['elec'=4,'pix'=8] {'pix'}, dimensions={0}, use_global_device_ids=true | all-gather | bytes 884736 | tf_op jit(solution)/shard_map/all_gather | solution.py:13
  221.6 5.5 %fusion.102 = f32[128,20480]{1,0:T(8,128)} fusion(bf16[384,20480]{1,0:T(8,128)(2,1)S(1)} %bitcast.207, bf16[384,64]{0,1:T(8,128)(2,1)S(1)} %get-tuple-element.7, bf16[384,64]{0,1:T(8,128)(2,1)S(1)} %get-tuple-element.8), kind=kOutput, calls=%fused_computation.129 | convolution fusion | flops 2013462528 | bytes 26312704 | tf_op jit(solution)/shard_map/dot_general | solution.py:33
  227.1 4.6 %slice_add_fusion = f32[64,20480]{1,0:T(8,128)S(1)} fusion(f32[128,20480]{1,0:T(8,128)} %fusion.102), kind=kLoop, calls=%fused_computation.8 | loop fusion | flops 1310720 | bytes 15728640 | tf_op jit(solution)/shard_map/add | solution.py:36
  232.0 1.7 pad_maximum_fusion.1
  233.7 34.4 %reduce-scatter.5.cloned.1.call-done = f32[2,32,2560]{2,1,0:T(8,128)} async-done(((f32[2,32,10240]{2,1,0:T(8,128)}), f32[2,32,2560]{2,1,0:T(8,128)}) %reduce-scatter.5.cloned.1.call-update) | async-done | bytes 655376 | tf_op jit(solution)/shard_map/reduce_scatter | solution.py:134
  268.1 2.0 fusion.165
  270.1 39.4 %psum.15 = f32[64,64]{1,0:T(8,128)S(1)} all-reduce(f32[64,64]{1,0:T(8,128)S(1)} %fusion.165), channel_id=1, replica_groups=mesh['elec'=4,'pix'=8] {'elec','pix'}, use_global_device_ids=true, to_apply=%region_6.7 | all-reduce | flops 4096 | bytes 32768 | tf_op jit(solution)/shard_map/psum | solution.py:137
  309.7 0.7 select_reduce_fusion
  310.4 0.9 fusion.45
  311.2 0.9 fusion.113
  317.1 1.3 copy.11
  318.4 4.0 all-to-all-start
  322.7 9.9 %all-to-all-done = f32[2,32,2560]{2,0,1:T(2,128)S(1)} async-done(((f32[2,32,2560]{2,0,1:T(2,128)}), f32[2,32,2560]{2,0,1:T(2,128)S(1)}, u32[]{:S(2)}, u32[]{:S(2)}) %all-to-all-start) | async-done | bytes 655392 | tf_op jit(solution)/shard_map/all_to_all | solution.py:140
  333.9 1.4 fusion.76
  335.3 1.4 fusion.72
  336.7 1.4 fusion.21
  338.2 1.4 fusion.20
  339.7 1.3 copy.14
  340.9 2.9 reshape.192
  343.8 5.4 %all-to-all-start.1 = ((f32[8,1,20480]{2,1,0:T(1,128)}), f32[8,1,20480]{2,1,0:T(1,128)S(1)}, u32[]{:S(2)}, u32[]{:S(2)}) async-start(f32[8,1,20480]{2,1,0:T(1,128)} %reshape.192), calls=%async_computation.3 | async-start | bytes 1310720 | tf_op jit(solution)/shard_map/all_to_all | solution.py:148
  349.5 16.7 %all-to-all-done.1 = f32[8,1,20480]{2,1,0:T(1,128)S(1)} async-done(((f32[8,1,20480]{2,1,0:T(1,128)}), f32[8,1,20480]{2,1,0:T(1,128)S(1)}, u32[]{:S(2)}, u32[]{:S(2)}) %all-to-all-start.1) | async-done | bytes 655392 | tf_op jit(solution)/shard_map/all_to_all | solution.py:148
  366.6 2.2 reduce
  368.8 3.0 reshape.193
  371.9 2.2 copy.18
  374.1 1.7 fusion.148
  375.8 1.9 copy.17
  378.0 2.8 fusion.59
  381.7 2.8 fusion.61
  384.5 2.8 fusion.18
  387.3 2.9 subtract_bitcast_fusion
  390.2 0.9 pad_maximum_fusion.2
  (100 shorter events, 14.0 us)
Async XLA Ops:
  6.5 98.9 %reduce-scatter.3.cloned.1.call-start = ((), (), s32[]{:S(2)}) async-start(), calls=%async_computation.4 | async-start | bytes 3276800 | tf_op jit(solution)/shard_map/reduce_scatter | solution.py:134
  6.5 11.1 %copy-start.3 = (f32[2,32,40,256]{3,2,1,0:T(8,128)S(1)}, f32[2,32,40,256]{3,2,1,0:T(8,128)}, u32[]{:S(2)}) copy-start(f32[2,32,40,256]{3,2,1,0:T(8,128)} %param.3) | copy-start | bytes 7864324
  17.7 40.0 %copy-start = (bf16[48,8,80,256]{3,1,2,0:T(8,128)(2,1)}, bf16[48,8,80,256]{3,1,2,0:T(8,128)(2,1)S(1)}, u32[]{:S(2)}) copy-start(bf16[48,8,80,256]{3,1,2,0:T(8,128)(2,1)S(1)} %copy.19) | copy-start | bytes 47185924
  69.9 105.8 %all-gather.4.cloned.1.call-start = ((), (), s32[]{:S(2)}) async-start(), calls=%async_computation.5 | async-start | bytes 1638400 | tf_op jit(solution)/shard_map/all_gather | solution.py:131
  153.9 67.6 %slice-start = ((s8[15728640]{0:T(1024)(128)(4,1)}), s8[3145728]{0:T(1024)(128)(4,1)S(1)}, s32[]{:S(2)}) async-start(s8[15728640]{0:T(1024)(128)(4,1)} %bitcast.205), calls=%async_computation.7 | async-start | bytes 6291456
  156.6 111.5 %reduce-scatter.5.cloned.1.call-start = ((), (), s32[]{:S(2)}) async-start(), calls=%async_computation.6 | async-start | bytes 3276800 | tf_op jit(solution)/shard_map/reduce_scatter | solution.py:134
  177.0 5.9 %copy-start.4 = (bf16[2,32,10240]{2,1,0:T(8,128)(2,1)S(1)}, bf16[2,32,10240]{2,1,0:T(8,128)(2,1)}, u32[]{:S(2)}) copy-start(bf16[2,32,10240]{2,1,0:T(8,128)(2,1)} %all-gather.4.cloned.1.call-done) | copy-start | bytes 3932164
  177.0 44.6 %slice-start.1 = ((s8[15728640]{0:T(1024)(128)(4,1)}), s8[4194304]{0:T(1024)(128)(4,1)S(1)}, s32[]{:S(2)}) async-start(s8[15728640]{0:T(1024)(128)(4,1)} %bitcast.205), calls=%async_computation.8 | async-start | bytes 8388608
  177.0 44.6 %slice-start.2 = ((s8[15728640]{0:T(1024)(128)(4,1)}), s8[4194304]{0:T(1024)(128)(4,1)S(1)}, s32[]{:S(2)}) async-start(s8[15728640]{0:T(1024)(128)(4,1)} %bitcast.205), calls=%async_computation.9 | async-start | bytes 8388608
  183.0 38.6 %slice-start.3 = ((s8[15728640]{0:T(1024)(128)(4,1)}), s8[4194304]{0:T(1024)(128)(4,1)S(1)}, s32[]{:S(2)}) async-start(s8[15728640]{0:T(1024)(128)(4,1)} %bitcast.205), calls=%async_computation.10 | async-start | bytes 8388608
  268.1 48.3 %copy-start.1 = (f32[2,32,2560]{2,1,0:T(8,128)S(1)}, f32[2,32,2560]{2,1,0:T(8,128)}, u32[]{:S(2)}) copy-start(f32[2,32,2560]{2,1,0:T(8,128)} %reduce-scatter.5.cloned.1.call-done) | copy-start | bytes 1966084
  318.4 14.2 %all-to-all-start = ((f32[2,32,2560]{2,0,1:T(2,128)}), f32[2,32,2560]{2,0,1:T(2,128)S(1)}, u32[]{:S(2)}, u32[]{:S(2)}) async-start(f32[2,32,2560]{2,0,1:T(2,128)} %copy.11), calls=%async_computation.2 | async-start | bytes 1310720 | tf_op jit(solution)/shard_map/all_to_all | solution.py:140
  343.8 22.3 %all-to-all-start.1 = ((f32[8,1,20480]{2,1,0:T(1,128)}), f32[8,1,20480]{2,1,0:T(1,128)S(1)}, u32[]{:S(2)}, u32[]{:S(2)}) async-start(f32[8,1,20480]{2,1,0:T(1,128)} %reshape.192), calls=%async_computation.3 | async-start | bytes 1310720 | tf_op jit(solution)/shard_map/all_to_all | solution.py:148
  375.8 5.0 %copy-start.2 = (f32[1,8,8,40,32]{4,2,3,1,0:T(8,128)S(1)}, f32[1,8,8,40,32]{4,2,3,1,0:T(8,128)}, u32[]{:S(2)}) copy-start(f32[1,8,8,40,32]{4,2,3,1,0:T(8,128)} %get-tuple-element.18) | copy-start | bytes 983044
Sparse Core Ops, SparseCore 0:
  70.0 35.4 reduce-scatter.2
  156.7 18.8 all-gather.3
  233.8 34.2 reduce-scatter.4
